TPU v7x, 32 devices: a whole 2x2x4 slice. The times are simulated.
32 devices in a mesh: line: 8 (over z, y), bus: 4 (over x, core).
Axes of the slice: x: 2, y: 2, z: 4, core: 2. Of those that a mesh axis runs over, the one named last changes fastest.
Arguments:
- clearness: float32 [192, 8192], P(None, ('line', 'bus')), may hold values from 0.05 to 0.8
- cos_zenith: float32 [192, 8192], P(None, ('line', 'bus')), may hold values from 0.05 to 1
- sun_azimuth: float32 [192, 8192], P(None, ('line', 'bus')), may hold values from -3.140625 to 3.140625
- dirint_cell: int32 [192, 8192], P(None, ('line', 'bus')), may hold values from 0 to 1259
- sky_bin: int32 [192, 8192], P(None, ('line', 'bus')), may hold values from 0 to 7
- dirint_coef: float32 [1260], replicated, may hold values from 0.5 to 1.5
- perez_coef: float32 [6, 8], replicated, may hold values from -0.3 to 0.6
- tilt_class: int32 [8192], P(('line', 'bus')), may hold values from 0 to 7
- azimuth_class: int32 [8192], P(('line', 'bus')), may hold values from 0 to 11
- tilt_table: float32 [8], replicated, may hold values from 0 to 1
- azimuth_table: float32 [12], replicated, may hold values from -3.140625 to 3.140625
- capacity: float32 [8192], P(('line', 'bus')), may hold values from 0.2 to 2
- site_bus: int32 [8192], P(('line', 'bus')), may hold values from 0 to 70143, as said below
- transfer_factors: bfloat16 [16000, 70144], P('line', 'bus'), may hold values from -0.0234375 to 0.0234375
Outputs:
- flows: float32 [16000, 192], P('line', 'bus')
Inputs may be any that keep to these rules, and one draw needn't show every extreme that they name: `site_bus`: bus b lies in group b // 2192. In every aligned block of 256 sites at most 16 sites connect to buses of one group, and one group receives exactly 16 sites from every block.
All inputs are finite; a program needn't handle non-finite values.
Results may differ from a plain program's by a relative error of at most 0.0034.
Values may be sent and summed in bfloat16 or wider, within the bound.
No kernel may reach another device: no remote copies, remote signals or barrier semaphores. Data moves between devices by JAX's collectives and lax.ppermute only.
A program may use at most 128 MiB of HBM per device.

v0:
```python
import math
import jax
import jax.numpy as jnp
from jax import lax
from jax.sharding import PartitionSpec as P

BUSES = 70144
TILTS = 8
AZIMS = 12
solar_constant = 1367.0
albedo = 0.2
cos_limit = 0.08716
row_width = 36


def pick_table(classes, table, count):
    picked = jnp.zeros(classes.shape, jnp.float32)
    for entry in range(count):
        picked = jnp.where(classes == entry, table[entry], picked)
    return picked


def dirint_lookup(cell, dirint_coef):
    row_count = dirint_coef.shape[0] // row_width
    table = dirint_coef.reshape(row_count, row_width)
    flat_cell = cell.reshape(-1)
    upper = flat_cell // row_width
    lower = flat_cell % row_width
    row_pick = (upper[:, None] == jnp.arange(row_count, dtype=jnp.int32)[None, :]).astype(
        jnp.float32
    )
    rows = jnp.dot(
        row_pick, table, precision=lax.Precision.HIGHEST, preferred_element_type=jnp.float32
    )
    column_hit = lower[:, None] == jnp.arange(row_width, dtype=jnp.int32)[None, :]
    picked = jnp.sum(jnp.where(column_hit, rows, 0.0), axis=1)
    return picked.reshape(cell.shape)


def site_power(
    clear,
    cosz,
    sun_az,
    cell,
    sky,
    tilt_angle,
    array_azimuth,
    site_capacity,
    dirint_coef,
    perez_coef,
):
    global_flat = clear * solar_constant * cosz
    zenith = jnp.arccos(cosz)
    airmass = 1.0 / (cosz + 0.50572 * (96.07995 - zenith * (180.0 / math.pi)) ** (-1.6364))
    clear_beam = (
        0.866 - 0.122 * airmass + 0.0121 * airmass**2 - 0.000653 * airmass**3 + 1.4e-05 * airmass**4
    )
    part_a = 0.512 - 1.56 * clear + 2.286 * clear**2 - 2.222 * clear**3
    part_b = 0.37 + 0.962 * clear
    part_c = -0.28 + 0.932 * clear - 2.048 * clear**2
    beam_index = jnp.maximum(clear_beam - (part_a + part_b * jnp.exp(part_c * airmass)), 0.0)
    direct_normal = solar_constant * beam_index * dirint_lookup(cell, dirint_coef)
    diffuse = jnp.maximum(global_flat - direct_normal * cosz, 0.1 * global_flat)
    brightness = diffuse * airmass / solar_constant
    factors = [jnp.zeros(cosz.shape, jnp.float32) for entry in range(6)]
    for bin_index in range(perez_coef.shape[1]):
        hit = sky == bin_index
        factors = [jnp.where(hit, perez_coef[row, bin_index], factors[row]) for row in range(6)]
    circumsolar = jnp.maximum(0.0, factors[0] + factors[1] * brightness + factors[2] * zenith)
    horizon_term = factors[3] + factors[4] * brightness + factors[5] * zenith
    cos_tilt = jnp.cos(tilt_angle)
    sin_tilt = jnp.sin(tilt_angle)
    cos_incidence = cosz * cos_tilt + jnp.sin(zenith) * sin_tilt * jnp.cos(sun_az - array_azimuth)
    facing = jnp.maximum(cos_incidence, 0.0)
    horizon_cos = jnp.maximum(cosz, cos_limit)
    sky_part = diffuse * (
        (1.0 - circumsolar) * (1.0 + cos_tilt) * 0.5
        + circumsolar * facing / horizon_cos
        + horizon_term * sin_tilt
    )
    plane = direct_normal * facing + sky_part + albedo * global_flat * (1.0 - cos_tilt) * 0.5
    return (site_capacity * plane / 1000.0).astype(jnp.bfloat16)


def per_device(
    clearness,
    cos_zenith,
    sun_azimuth,
    dirint_cell,
    sky_bin,
    dirint_coef,
    perez_coef,
    tilt_class,
    azimuth_class,
    tilt_table,
    azimuth_table,
    capacity,
    site_bus,
    transfer_factors,
):
    line_count = lax.axis_size("line")
    bus_count = lax.axis_size("bus")
    owners = line_count * bus_count
    n_hours, n_sites = clearness.shape
    group_buses = BUSES // owners
    slots_each = max(2, 2 * n_sites // owners)
    tilt_angle = pick_table(tilt_class, tilt_table, TILTS)
    array_azimuth = pick_table(azimuth_class, azimuth_table, AZIMS)
    power = site_power(
        clearness,
        cos_zenith,
        sun_azimuth,
        dirint_cell,
        sky_bin,
        tilt_angle,
        array_azimuth,
        capacity,
        dirint_coef,
        perez_coef,
    )
    group_index = site_bus // group_buses
    target = group_index % line_count * bus_count + group_index // line_count
    local_bus = site_bus % group_buses
    one_hot = (target[:, None] == jnp.arange(owners, dtype=jnp.int32)[None, :]).astype(jnp.int32)
    position = jnp.sum(one_hot * (jnp.cumsum(one_hot, axis=0) - 1), axis=1)
    slot_index = target * slots_each + position
    outgoing = jnp.zeros((n_hours, owners * slots_each), jnp.bfloat16).at[:, slot_index].set(power)
    labels = jnp.zeros((1, owners * slots_each), jnp.int32).at[0, slot_index].set(local_bus)
    arrived, bus_tags = (
        lax.all_to_all(outgoing, ("line", "bus"), split_axis=1, concat_axis=1, tiled=True),
        lax.all_to_all(labels, ("line", "bus"), split_axis=1, concat_axis=1, tiled=True),
    )
    bus_tags = bus_tags.reshape(owners * slots_each)
    member = (bus_tags[:, None] == jnp.arange(group_buses, dtype=jnp.int32)[None, :]).astype(
        jnp.bfloat16
    )
    injection = jnp.einsum("hr,rb->bh", arrived, member, preferred_element_type=jnp.float32).astype(
        jnp.bfloat16
    )
    partial_flows = jnp.dot(
        transfer_factors,
        lax.all_gather(injection, "line", axis=0, tiled=True),
        preferred_element_type=jnp.float32,
    )
    return lax.psum_scatter(partial_flows, "bus", scatter_dimension=1, tiled=True)


def solution(mesh):
    in_specs = (
        P(None, ("line", "bus")),
        P(None, ("line", "bus")),
        P(None, ("line", "bus")),
        P(None, ("line", "bus")),
        P(None, ("line", "bus")),
        P(),
        P(),
        P(("line", "bus")),
        P(("line", "bus")),
        P(),
        P(),
        P(("line", "bus")),
        P(("line", "bus")),
        P("line", "bus"),
    )
    out_specs = P("line", "bus")
    return jax.shard_map(
        per_device, mesh=mesh, in_specs=in_specs, out_specs=out_specs, check_vma=False
    )
```

profile of v0, /device:TPU:0, one launch (start us, length us, event | category | flops | bytes accessed | tf_op | source)
XLA Modules:
  0.0 296.3 jit_solution(16229938110226175644)
XLA Ops:
  6.5 0.0 copy-start.4
  6.5 0.0 copy-start.5
  6.5 0.0 copy-start.1
  6.5 0.0 copy-start.3
  6.5 0.0 copy-start
  6.5 0.0 copy-start.2
  6.6 0.8 and_select_fusion
  7.3 0.6 reduce-window.6
  7.9 0.2 slice_reduce_fusion
  8.2 0.1 fusion.27
  8.3 1.4 scatter_custom_fusion
  9.7 0.7 all_to_all.14
  10.4 7.3 %all-to-all-start = ((s32[1,32,16]{2,0,1:T(1,128)}), s32[1,32,16]{2,0,1:T(1,128)S(1)}, u32[]{:S(2)}, u32[]{:S(2)}) async-start(s32[1,32,16]{2,0,1:T(1,128)} %bitcast.2), calls=%async_computation | async-start | bytes 32768 | tf_op jit(solution)/shard_map/all_to_all | solution.py:131
  17.7 1.7 fusion.36
  19.4 2.1 fusion.34
  21.5 2.1 fusion.35
  23.6 1.0 sign_compare_fusion
  24.6 1.0 remainder_bitcast_fusion
  25.6 1.6 fusion.38
  27.2 5.7 %fusion.33 = (f32[256]{0:T(256)S(1)}, f32[256]{0:T(256)S(1)}) fusion(f32[]{:T(128)} %bitcast.10, s32[256]{0:T(256)} %param.21, f32[]{:T(128)} %bitcast.9, f32[]{:T(128)} %bitcast.8, f32[]{:T(128)} %bitcast.7, f32[]{:T(128)} %bitcast.6, f32[]{:T(128)} %bitcast.5, f32[]{:T(128)} %bitcast.4, f32[]{:T(128)} %bitcast.3), kind=kLoop, calls=%fused_computation.89 | loop fusion | flops 4096 | bytes 3104 | tf_op jit(solution)/shard_map/sin | solution.py:72
  33.0 1.8 fusion.37
  34.8 0.8 reshape.70
  35.7 0.1 copy.28
  35.8 0.1 copy.29
  35.9 0.1 add_select_fusion.1
  36.0 5.6 %fusion.5 = f32[49152]{0:T(1024)S(1)} fusion(f32[35,36]{1,0:T(8,128)S(1)} %reshape.70, s32[49152]{0:T(1024)S(1)} %get-tuple-element.8, s32[49152]{0:T(1024)S(1)} %get-tuple-element.7), kind=kOutput, calls=%fused_computation.12 | convolution fusion | flops 750157824 | bytes 594864 | tf_op jit(solution)/shard_map/dot_general | solution.py:32
  41.6 0.1 reshape.71
  41.7 0.0 copy-done.4
  41.7 7.5 %broadcast_add_fusion = (f32[256]{0:T(256)S(1)}, f32[256]{0:T(256)S(1)}, f32[256]{0:T(256)S(1)}) fusion(f32[256]{0:T(256)S(1)} %cos.6, f32[]{:T(128)} %bitcast.22, s32[256]{0:T(256)S(1)} %copy-done.4, f32[]{:T(128)} %bitcast.21, f32[]{:T(128)} %bitcast.20, f32[]{:T(128)} %bitcast.19, f32[]{:T(128)} %bitcast.18, f32[]{:T(128)} %bitcast.17, f32[]{:T(128)} %bitcast.16, ...), kind=kLoop, calls=%fused_computation.88 | loop fusion | flops 6912 | bytes 5168 | tf_op jit(solution)/shard_map/add | solution.py:77
  49.2 0.0 copy-done.5
  49.2 0.0 copy-done.1
  49.2 0.0 copy-done.3
  49.2 0.0 copy-done
  49.3 0.0 copy-done.2
  49.3 32.6 %fusion.25 = bf16[256,192]{0,1:T(8,128)(2,1)S(1)} fusion(f32[256]{0:T(256)S(1)} %get-tuple-element.62, f32[]{:T(128)} %bitcast.70, f32[]{:T(128)} %bitcast.69, f32[]{:T(128)} %bitcast.68, f32[]{:T(128)} %bitcast.67, f32[]{:T(128)} %bitcast.66, f32[]{:T(128)} %bitcast.65, f32[]{:T(128)} %bitcast.64, f32[]{:T(128)} %bitcast.63, f32[]{:T(128)} %bitcast.62, ...), kind=kLoop, calls=%fused_computation.45 | loop fusion | flops 6733824 | bytes 1087680 | tf_op jit(solution)/shard_map/convert_element_type | solution.py:82
  81.8 0.1 copy.25
  81.9 2.1 scatter_custom_fusion.1
  84.1 0.0 all-to-all-done
  84.1 5.8 %all-to-all-start.1 = ((bf16[192,32,16]{0,2,1:T(8,128)(2,1)}), bf16[192,32,16]{0,2,1:T(8,128)(2,1)S(1)}, u32[]{:S(2)}, u32[]{:S(2)}) async-start(bf16[192,32,16]{0,2,1:T(8,128)(2,1)} %bitcast.72), calls=%async_computation.1 | async-start | bytes 524288 | tf_op jit(solution)/shard_map/all_to_all | solution.py:130
  89.9 0.0 all-gather.3.cloned.1.call-start
  90.0 0.5 broadcast.198
  90.5 0.7 reduce.5
  91.2 0.1 eq.192
  91.3 9.2 %all-to-all-done.1 = bf16[192,32,16]{0,2,1:T(8,128)(2,1)S(1)} async-done(((bf16[192,32,16]{0,2,1:T(8,128)(2,1)}), bf16[192,32,16]{0,2,1:T(8,128)(2,1)S(1)}, u32[]{:S(2)}, u32[]{:S(2)}) %all-to-all-start.1) | async-done | bytes 196640 | tf_op jit(solution)/shard_map/all_to_all | solution.py:130
  100.5 2.1 fusion.3
  102.6 0.0 all-gather.3.cloned.1.call-update
  102.7 0.2 reduce-scatter.2.cloned.1.call-start
  102.9 106.5 %all-gather.3.cloned.1.call-done = bf16[8,2192,192]{1,2,0:T(8,128)(2,1)} async-done(((bf16[1,2192,192]{1,2,0:T(8,128)(2,1)}), bf16[8,2192,192]{1,2,0:T(8,128)(2,1)}) %all-gather.3.cloned.1.call-update) | async-done | bytes 6733840 | tf_op jit(solution)/shard_map/all_gather | solution.py:142
  209.4 9.8 %copy.26 = bf16[8,2192,192]{1,0,2:T(8,128)(2,1)} copy(bf16[8,2192,192]{1,2,0:T(8,128)(2,1)} %all-gather.3.cloned.1.call-done) | data formatting | bytes 13467648 | tf_op jit(solution)/shard_map/all_gather | solution.py:142
  219.3 12.5 %reshape.97 = bf16[17536,192]{0,1:T(8,128)(2,1)} reshape(bf16[8,2192,192]{1,0,2:T(8,128)(2,1)} %copy.26) | data formatting | bytes 13467648
  231.8 31.1 %convolution_bitcast_fusion = f32[2000,192]{0,1:T(8,128)} fusion(bf16[17536,192]{0,1:T(8,128)(2,1)} %reshape.97, bf16[2000,17536]{1,0:T(8,128)(2,1)} %param.27), kind=kOutput, calls=%fused_computation.10 | convolution fusion | flops 13467648000 | bytes 78413824 | tf_op jit(solution)/shard_map/dot_general | solution.py:140
  262.9 0.0 reduce-scatter.2.cloned.1.call-update
  262.9 26.5 %reduce-scatter.2.cloned.1.call-done = f32[2000,48]{0,1:T(8,128)} async-done(((f32[2000,192]{0,1:T(8,128)}), f32[2000,48]{0,1:T(8,128)}) %reduce-scatter.2.cloned.1.call-update) | async-done | bytes 384016 | tf_op jit(solution)/shard_map/reduce_scatter | solution.py:145
  (6 shorter events, 0.1 us)
Async XLA Ops:
  6.5 35.2 %copy-start.4 = (s32[256]{0:T(256)S(1)}, s32[256]{0:T(256)}, u32[]{:S(2)}) copy-start(s32[256]{0:T(256)} %param.22) | copy-start | bytes 3076
  6.5 42.7 %copy-start.5 = (f32[256]{0:T(256)S(1)}, f32[256]{0:T(256)}, u32[]{:S(2)}) copy-start(f32[256]{0:T(256)} %param.25) | copy-start | bytes 3076
  6.5 42.7 %copy-start.1 = (s32[192,256]{1,0:T(8,128)S(1)}, s32[192,256]{1,0:T(8,128)}, u32[]{:S(2)}) copy-start(s32[192,256]{1,0:T(8,128)} %param.18) | copy-start | bytes 589828
  6.5 42.7 %copy-start.3 = (f32[192,256]{1,0:T(8,128)S(1)}, f32[192,256]{1,0:T(8,128)}, u32[]{:S(2)}) copy-start(f32[192,256]{1,0:T(8,128)} %param.16) | copy-start | bytes 589828
  6.5 42.7 %copy-start = (f32[192,256]{1,0:T(8,128)S(1)}, f32[192,256]{1,0:T(8,128)}, u32[]{:S(2)}) copy-start(f32[192,256]{1,0:T(8,128)} %param.15) | copy-start | bytes 589828
  6.5 42.7 %copy-start.2 = (f32[192,256]{1,0:T(8,128)S(1)}, f32[192,256]{1,0:T(8,128)}, u32[]{:S(2)}) copy-start(f32[192,256]{1,0:T(8,128)} %param.14) | copy-start | bytes 589828
  10.4 73.7 %all-to-all-start = ((s32[1,32,16]{2,0,1:T(1,128)}), s32[1,32,16]{2,0,1:T(1,128)S(1)}, u32[]{:S(2)}, u32[]{:S(2)}) async-start(s32[1,32,16]{2,0,1:T(1,128)} %bitcast.2), calls=%async_computation | async-start | bytes 32768 | tf_op jit(solution)/shard_map/all_to_all | solution.py:131
  84.1 16.4 %all-to-all-start.1 = ((bf16[192,32,16]{0,2,1:T(8,128)(2,1)}), bf16[192,32,16]{0,2,1:T(8,128)(2,1)S(1)}, u32[]{:S(2)}, u32[]{:S(2)}) async-start(bf16[192,32,16]{0,2,1:T(8,128)(2,1)} %bitcast.72), calls=%async_computation.1 | async-start | bytes 524288 | tf_op jit(solution)/shard_map/all_to_all | solution.py:130
  89.9 119.5 %all-gather.3.cloned.1.call-start = ((), (), s32[]{:S(2)}) async-start(), calls=%async_computation.4 | async-start | bytes 7962624 | tf_op jit(solution)/shard_map/all_gather | solution.py:142
  102.7 186.8 %reduce-scatter.2.cloned.1.call-start = ((), (), s32[]{:S(2)}) async-start(), calls=%async_computation.3 | async-start | bytes 1966080 | tf_op jit(solution)/shard_map/reduce_scatter | solution.py:145
Sparse Core Ops, SparseCore 0:
  102.8 106.5 all-gather.2
  263.0 26.3 reduce-scatter.1
where the time goes:
time: 298 us; the launch traced here: 296 us
  waiting for transfers between devices  142 us (48%)
  other arithmetic  50.1 us (17%)
  matrix products  38.8 us (13%)
  local copies, waits for them, and re-layouts  38 us (13%)
  between operations  13.6 us (5%)
  starting transfers between devices  13.4 us (4%)
    all_gather x1, waiting for transfers between devices, per_device(): lax.all_gather(injection, 'line', axis=0, tiled=True)  107 us
    convert_element_type x1, other arithmetic, site_power(): return (site_capacity * plane / 1000.0).astype(jnp.bfloat16)  32.6 us
    dot_general x1, matrix products, per_device(): jnp.dot(transfer_factors, lax.all_gather(injection, 'line', axis=0, tiled...  31.1 us
    reduce_scatter x1, waiting for transfers between devices, per_device(): lax.psum_scatter(partial_flows, 'bus', scatter_dimension=1, tiled=True)  26.5 us
    unnamed x15, local copies, waits for them, and re-layouts  12.8 us
    all_gather x1, local copies, waits for them, and re-layouts, per_device(): lax.all_gather(injection, 'line', axis=0, tiled=True)  9.83 us
    all_to_all x1, waiting for transfers between devices, per_device(): lax.all_to_all(outgoing, ('line', 'bus'), split_axis=1, concat_axis=1, ti...  9.25 us
    add x1, other arithmetic, site_power(): 1.0 + cos_tilt  7.51 us
  transfers between devices with their start and end apart: 4, of which 3 were waited for; matrix products, arithmetic and copies ran while one was open for 23% of the time, Pallas kernels for 0%

commit v1 on v0

--- a/solution.py
+++ b/solution.py
@@ -11,6 +11,12 @@
 albedo = 0.2
 cos_limit = 0.08716
 row_width = 36
+
+
+def exchange_blocks(x, mesh_axis, split, join):
+    pieces = jnp.split(x, lax.axis_size(mesh_axis), axis=split)
+    got = lax.all_to_all(jnp.stack(pieces), mesh_axis, 0, 0)
+    return jnp.concatenate(got, axis=join)
 
 
 def pick_table(classes, table, count):
@@ -128,7 +134,7 @@
     labels = jnp.zeros((1, owners * slots_each), jnp.int32).at[0, slot_index].set(local_bus)
     arrived, bus_tags = (
         lax.all_to_all(outgoing, ("line", "bus"), split_axis=1, concat_axis=1, tiled=True),
-        lax.all_to_all(labels, ("line", "bus"), split_axis=1, concat_axis=1, tiled=True),
+        exchange_blocks(labels, ("line", "bus"), 1, 1),
     )
     bus_tags = bus_tags.reshape(owners * slots_each)
     member = (bus_tags[:, None] == jnp.arange(group_buses, dtype=jnp.int32)[None, :]).astype(

time: 298 us -> 316 us (1.060)
  local copies, waits for them, and re-layouts: 38 us -> 56.6 us
    unnamed x15 -> x46, local copies, waits for them, and re-layouts: 12.8 us -> 31.4 us
  transfers between devices with their start and end apart: 4 -> 4, of which waited for: 3 -> 3; matrix products, arithmetic and copies ran while one was open for 23% -> 21% of each run, Pallas kernels for 0% -> 0%
where the time goes in v1:
time: 316 us; the launch traced here: 315 us
  waiting for transfers between devices  142 us (45%)
  local copies, waits for them, and re-layouts  56.6 us (18%)
  other arithmetic  50.1 us (16%)
  matrix products  38.8 us (12%)
  between operations  13.6 us (4%)
  starting transfers between devices  13.4 us (4%)
    all_gather x1, waiting for transfers between devices, per_device(): lax.all_gather(injection, 'line', axis=0, tiled=True)  107 us
    convert_element_type x1, other arithmetic, site_power(): return (site_capacity * plane / 1000.0).astype(jnp.bfloat16)  32.6 us
    unnamed x46, local copies, waits for them, and re-layouts  31.4 us
    dot_general x1, matrix products, per_device(): jnp.dot(transfer_factors, lax.all_gather(injection, 'line', axis=0, tiled...  31.1 us
    reduce_scatter x1, waiting for transfers between devices, per_device(): lax.psum_scatter(partial_flows, 'bus', scatter_dimension=1, tiled=True)  26.5 us
    all_gather x1, local copies, waits for them, and re-layouts, per_device(): lax.all_gather(injection, 'line', axis=0, tiled=True)  9.83 us
    all_to_all x1, waiting for transfers between devices, per_device(): lax.all_to_all(outgoing, ('line', 'bus'), split_axis=1, concat_axis=1, ti...  9.25 us
    add x1, other arithmetic, site_power(): 1.0 + cos_tilt  7.51 us
  transfers between devices with their start and end apart: 4, of which 3 were waited for; matrix products, arithmetic and copies ran while one was open for 21% of the time, Pallas kernels for 0%

profile of v1, /device:TPU:0, one launch (start us, length us, event | category | flops | bytes accessed | tf_op | source)
XLA Modules:
  0.0 314.9 jit_solution(11302072933500012389)
XLA Ops:
  6.6 0.8 and_select_fusion
  7.3 0.6 reduce-window.6
  7.9 0.2 slice_reduce_fusion
  8.2 0.1 fusion.27
  8.3 1.4 scatter_custom_fusion
  9.7 0.5 constant_dynamic-update-slice_fusion.31
  10.2 0.6 constant_dynamic-update-slice_fusion.30
  10.9 0.6 constant_dynamic-update-slice_fusion.29
  11.5 0.6 constant_dynamic-update-slice_fusion.28
  12.1 0.6 constant_dynamic-update-slice_fusion.27
  12.7 0.6 constant_dynamic-update-slice_fusion.26
  13.3 0.6 constant_dynamic-update-slice_fusion.25
  13.9 0.7 constant_dynamic-update-slice_fusion.24
  14.5 0.5 constant_dynamic-update-slice_fusion.23
  15.1 0.6 constant_dynamic-update-slice_fusion.22
  15.7 0.6 constant_dynamic-update-slice_fusion.21
  16.3 0.6 constant_dynamic-update-slice_fusion.20
  16.9 0.6 constant_dynamic-update-slice_fusion.19
  17.5 0.7 constant_dynamic-update-slice_fusion.18
  18.2 0.6 constant_dynamic-update-slice_fusion.17
  18.8 0.6 constant_dynamic-update-slice_fusion.16
  19.4 0.6 constant_dynamic-update-slice_fusion.15
  20.0 0.5 constant_dynamic-update-slice_fusion.14
  20.5 0.6 constant_dynamic-update-slice_fusion.13
  21.1 0.7 constant_dynamic-update-slice_fusion.12
  21.8 0.6 constant_dynamic-update-slice_fusion.11
  22.4 0.6 constant_dynamic-update-slice_fusion.10
  23.0 0.6 constant_dynamic-update-slice_fusion.9
  23.6 0.6 constant_dynamic-update-slice_fusion.8
  24.2 0.5 constant_dynamic-update-slice_fusion.7
  24.7 0.6 constant_dynamic-update-slice_fusion.6
  25.4 0.6 constant_dynamic-update-slice_fusion.5
  26.0 0.6 constant_dynamic-update-slice_fusion.4
  26.5 0.7 constant_dynamic-update-slice_fusion.3
  27.2 0.6 constant_dynamic-update-slice_fusion.2
  27.8 0.6 constant_dynamic-update-slice_fusion.1
  28.4 0.6 constant_dynamic-update-slice_fusion
  29.0 7.3 %all-to-all-start = ((s32[32,1,16]{2,1,0:T(1,128)}), s32[32,1,16]{2,1,0:T(1,128)S(1)}, u32[]{:S(2)}, u32[]{:S(2)}) async-start(s32[32,1,16]{2,1,0:T(1,128)} %constant_dynamic-update-slice_fusion), calls=%async_computation | async-start | bytes 32768 | tf_op jit(solution)/shard_map/all_to_all | solution.py:18
  36.3 1.7 fusion.36
  38.0 2.1 fusion.34
  40.1 2.1 fusion.35
  42.2 1.0 sign_compare_fusion
  43.2 1.0 remainder_bitcast_fusion
  44.2 1.6 fusion.38
  45.9 5.7 %fusion.33 = (f32[256]{0:T(256)S(1)}, f32[256]{0:T(256)S(1)}) fusion(f32[]{:T(128)} %bitcast.42, s32[256]{0:T(256)} %param.21, f32[]{:T(128)} %bitcast.41, f32[]{:T(128)} %bitcast.40, f32[]{:T(128)} %bitcast.39, f32[]{:T(128)} %bitcast.38, f32[]{:T(128)} %bitcast.37, f32[]{:T(128)} %bitcast.36, f32[]{:T(128)} %bitcast.35), kind=kLoop, calls=%fused_computation.153 | loop fusion | flops 4096 | bytes 3104 | tf_op jit(solution)/shard_map/sin | solution.py:78
  51.7 1.8 fusion.37
  53.4 0.8 reshape.67
  54.3 0.1 copy.26
  54.4 0.1 copy.27
  54.6 5.6 %fusion.5 = f32[49152]{0:T(1024)S(1)} fusion(f32[35,36]{1,0:T(8,128)S(1)} %reshape.67, s32[49152]{0:T(1024)S(1)} %get-tuple-element.8, s32[49152]{0:T(1024)S(1)} %get-tuple-element.7), kind=kOutput, calls=%fused_computation.12 | convolution fusion | flops 750157824 | bytes 594864 | tf_op jit(solution)/shard_map/dot_general | solution.py:38
  60.3 7.5 %broadcast_add_fusion = (f32[256]{0:T(256)S(1)}, f32[256]{0:T(256)S(1)}, f32[256]{0:T(256)S(1)}) fusion(f32[256]{0:T(256)S(1)} %cos.6, f32[]{:T(128)} %bitcast.54, s32[256]{0:T(256)S(1)} %copy-done.4, f32[]{:T(128)} %bitcast.53, f32[]{:T(128)} %bitcast.52, f32[]{:T(128)} %bitcast.51, f32[]{:T(128)} %bitcast.50, f32[]{:T(128)} %bitcast.49, f32[]{:T(128)} %bitcast.48, ...), kind=kLoop, calls=%fused_computation.152 | loop fusion | flops 6912 | bytes 5168 | tf_op jit(solution)/shard_map/add | solution.py:83
  67.9 32.6 %fusion.25 = bf16[256,192]{0,1:T(8,128)(2,1)S(1)} fusion(f32[256]{0:T(256)S(1)} %get-tuple-element.62, f32[]{:T(128)} %bitcast.102, f32[]{:T(128)} %bitcast.101, f32[]{:T(128)} %bitcast.100, f32[]{:T(128)} %bitcast.99, f32[]{:T(128)} %bitcast.98, f32[]{:T(128)} %bitcast.97, f32[]{:T(128)} %bitcast.96, f32[]{:T(128)} %bitcast.95, f32[]{:T(128)} %bitcast.94, ...), kind=kLoop, calls=%fused_computation.45 | loop fusion | flops 6733824 | bytes 1087680 | tf_op jit(solution)/shard_map/convert_element_type | solution.py:88
  100.6 2.1 scatter_custom_fusion.1
  102.7 5.8 %all-to-all-start.1 = ((bf16[192,32,16]{0,2,1:T(8,128)(2,1)}), bf16[192,32,16]{0,2,1:T(8,128)(2,1)S(1)}, u32[]{:S(2)}, u32[]{:S(2)}) async-start(bf16[192,32,16]{0,2,1:T(8,128)(2,1)} %bitcast.104), calls=%async_computation.1 | async-start | bytes 524288 | tf_op jit(solution)/shard_map/all_to_all | solution.py:136
  108.6 0.5 broadcast.198
  109.1 0.7 reduce.5
  109.9 9.2 %all-to-all-done.1 = bf16[192,32,16]{0,2,1:T(8,128)(2,1)S(1)} async-done(((bf16[192,32,16]{0,2,1:T(8,128)(2,1)}), bf16[192,32,16]{0,2,1:T(8,128)(2,1)S(1)}, u32[]{:S(2)}, u32[]{:S(2)}) %all-to-all-start.1) | async-done | bytes 196640 | tf_op jit(solution)/shard_map/all_to_all | solution.py:136
  119.1 2.1 fusion.3
  121.3 0.2 reduce-scatter.2.cloned.1.call-start
  121.5 106.5 %all-gather.3.cloned.1.call-done = bf16[8,2192,192]{1,2,0:T(8,128)(2,1)} async-done(((bf16[1,2192,192]{1,2,0:T(8,128)(2,1)}), bf16[8,2192,192]{1,2,0:T(8,128)(2,1)}) %all-gather.3.cloned.1.call-update) | async-done | bytes 6733840 | tf_op jit(solution)/shard_map/all_gather | solution.py:148
  228.0 9.8 %copy.24 = bf16[8,2192,192]{1,0,2:T(8,128)(2,1)} copy(bf16[8,2192,192]{1,2,0:T(8,128)(2,1)} %all-gather.3.cloned.1.call-done) | data formatting | bytes 13467648 | tf_op jit(solution)/shard_map/all_gather | solution.py:148
  237.9 12.5 %reshape.93 = bf16[17536,192]{0,1:T(8,128)(2,1)} reshape(bf16[8,2192,192]{1,0,2:T(8,128)(2,1)} %copy.24) | data formatting | bytes 13467648
  250.4 31.1 %convolution_bitcast_fusion = f32[2000,192]{0,1:T(8,128)} fusion(bf16[17536,192]{0,1:T(8,128)(2,1)} %reshape.93, bf16[2000,17536]{1,0:T(8,128)(2,1)} %param.27), kind=kOutput, calls=%fused_computation.10 | convolution fusion | flops 13467648000 | bytes 78413824 | tf_op jit(solution)/shard_map/dot_general | solution.py:146
  281.5 26.5 %reduce-scatter.2.cloned.1.call-done = f32[2000,48]{0,1:T(8,128)} async-done(((f32[2000,192]{0,1:T(8,128)}), f32[2000,48]{0,1:T(8,128)}) %reduce-scatter.2.cloned.1.call-update) | async-done | bytes 384016 | tf_op jit(solution)/shard_map/reduce_scatter | solution.py:151
  (26 shorter events, 0.6 us)
Async XLA Ops:
  6.5 53.8 %copy-start.4 = (s32[256]{0:T(256)S(1)}, s32[256]{0:T(256)}, u32[]{:S(2)}) copy-start(s32[256]{0:T(256)} %param.22) | copy-start | bytes 3076
  6.5 61.3 %copy-start.5 = (f32[256]{0:T(256)S(1)}, f32[256]{0:T(256)}, u32[]{:S(2)}) copy-start(f32[256]{0:T(256)} %param.25) | copy-start | bytes 3076
  6.5 61.3 %copy-start.1 = (s32[192,256]{1,0:T(8,128)S(1)}, s32[192,256]{1,0:T(8,128)}, u32[]{:S(2)}) copy-start(s32[192,256]{1,0:T(8,128)} %param.18) | copy-start | bytes 589828
  6.5 61.3 %copy-start.3 = (f32[192,256]{1,0:T(8,128)S(1)}, f32[192,256]{1,0:T(8,128)}, u32[]{:S(2)}) copy-start(f32[192,256]{1,0:T(8,128)} %param.16) | copy-start | bytes 589828
  6.5 61.3 %copy-start = (f32[192,256]{1,0:T(8,128)S(1)}, f32[192,256]{1,0:T(8,128)}, u32[]{:S(2)}) copy-start(f32[192,256]{1,0:T(8,128)} %param.15) | copy-start | bytes 589828
  6.5 61.3 %copy-start.2 = (f32[192,256]{1,0:T(8,128)S(1)}, f32[192,256]{1,0:T(8,128)}, u32[]{:S(2)}) copy-start(f32[192,256]{1,0:T(8,128)} %param.14) | copy-start | bytes 589828
  29.0 73.7 %all-to-all-start = ((s32[32,1,16]{2,1,0:T(1,128)}), s32[32,1,16]{2,1,0:T(1,128)S(1)}, u32[]{:S(2)}, u32[]{:S(2)}) async-start(s32[32,1,16]{2,1,0:T(1,128)} %constant_dynamic-update-slice_fusion), calls=%async_computation | async-start | bytes 32768 | tf_op jit(solution)/shard_map/all_to_all | solution.py:18
  102.7 16.4 %all-to-all-start.1 = ((bf16[192,32,16]{0,2,1:T(8,128)(2,1)}), bf16[192,32,16]{0,2,1:T(8,128)(2,1)S(1)}, u32[]{:S(2)}, u32[]{:S(2)}) async-start(bf16[192,32,16]{0,2,1:T(8,128)(2,1)} %bitcast.104), calls=%async_computation.1 | async-start | bytes 524288 | tf_op jit(solution)/shard_map/all_to_all | solution.py:136
  108.5 119.5 %all-gather.3.cloned.1.call-start = ((), (), s32[]{:S(2)}) async-start(), calls=%async_computation.4 | async-start | bytes 7962624 | tf_op jit(solution)/shard_map/all_gather | solution.py:148
  121.3 186.8 %reduce-scatter.2.cloned.1.call-start = ((), (), s32[]{:S(2)}) async-start(), calls=%async_computation.3 | async-start | bytes 1966080 | tf_op jit(solution)/shard_map/reduce_scatter | solution.py:151
Sparse Core Ops, SparseCore 0:
  121.4 106.5 all-gather.2
  281.6 26.3 reduce-scatter.1
